TPU v7x, 32 devices: a whole 2x2x4 slice. The times are simulated.
32 devices in a mesh: dp: 4 (over z), adapter: 8 (over y, x, core).
Axes of the slice: x: 2, y: 2, z: 4, core: 2. Of those that a mesh axis runs over, the one named last changes fastest.
Arguments:
- states: bfloat16 [2, 1024, 8192], P(None, ('dp', 'adapter')), may hold values from -6 to 6
- request_slot_index: int32 [2, 1024, 1], P(None, ('dp', 'adapter')), may hold values from 0 to 7; in each aligned block of 32 rows (0 to 31, 32 to 63, ..., all dimensions but the last counted through in order) at most 8 rows name the same one
- down_weights: bfloat16 [32, 64, 8192], P(('dp', 'adapter')), may hold values from -0.0625 to 0.0625
- up_weights: bfloat16 [32, 64, 8192], P(('dp', 'adapter')), may hold values from -0.75 to 0.75
- active_adapter_owner: int32 [2, 8], replicated, may hold values from 0 to 3
Outputs:
- delta: bfloat16 [2, 1024, 8192], P(None, ('dp', 'adapter'))
Inputs may be any that keep to these rules, and one draw needn't show every extreme that they name: `request_slot_index`: within the rows of one device at one step (aligned blocks of 32 rows), no column is named by more than 8 rows, a bound that some block reaches.
All inputs are finite; a program needn't handle non-finite values.
Results may differ from a plain program's by a relative error of at most 0.0049.
Values may be sent and summed in bfloat16 or wider, within the bound.
A program may use at most 64 MiB of HBM per device.

v0:
```python
import jax
import jax.numpy as jnp
from jax import lax
from jax.sharding import PartitionSpec as P


def from_root(array, axis, root):
    mine = lax.axis_index(axis) == root
    return lax.psum(jnp.where(mine, array, jnp.zeros_like(array)), axis)


def slot_matrix(column_ids, columns, capacity):
    hits = (column_ids[:, None] == jnp.arange(columns, dtype=jnp.int32)[None, :]).astype(jnp.int32)
    slot_rank = jnp.sum(jnp.cumsum(hits, axis=0) * hits, axis=1) - 1
    target = column_ids * capacity + slot_rank
    return (target[:, None] == jnp.arange(columns * capacity, dtype=jnp.int32)[None, :]).astype(
        jnp.bfloat16
    )


def project(arrived, stack_down, stack_up):
    low_rank = jnp.einsum(
        "scnd,srd->scnr", arrived, stack_down, preferred_element_type=jnp.float32
    ).astype(jnp.bfloat16)
    return jnp.einsum(
        "scnr,srd->scnd", low_rank, stack_up, preferred_element_type=jnp.float32
    ).astype(jnp.bfloat16)


def serve_one(arrived, stack_down, stack_up):
    result = project(arrived, stack_down, stack_up)
    return lax.all_to_all(result, "adapter", split_axis=1, concat_axis=1, tiled=True)


def body(states, request_slot_index, down_weights, up_weights, active_adapter_owner):
    step_count = states.shape[0]
    rows_dev = states.shape[1]
    model_width = states.shape[2]
    columns = lax.axis_size("adapter")
    column_index = lax.axis_index("adapter")
    capacity = max(2, 2 * rows_dev // columns)
    slot_count = columns * capacity
    downs = []
    uppers = []
    for step_index in range(step_count):
        owner_leader = active_adapter_owner[step_index, column_index]
        got_down, got_up = (
            from_root(down_weights[0], "dp", owner_leader),
            from_root(up_weights[0], "dp", owner_leader),
        )
        downs.append(got_down)
        uppers.append(got_up)
    stack_down = jnp.stack(downs)
    stack_up = jnp.stack(uppers)
    placements = []
    outgoing_list = []
    for step_index in range(step_count):
        placement = slot_matrix(request_slot_index[step_index, :, 0], columns, capacity)
        placements.append(placement)
        packed = lax.dot_general(
            placement,
            states[step_index],
            (((0,), (0,)), ((), ())),
            preferred_element_type=jnp.float32,
        )
        outgoing_list.append(packed.astype(jnp.bfloat16).reshape(columns, capacity, model_width))
    outgoing = jnp.stack(outgoing_list)
    returned_list = []
    for step_index in range(step_count):
        returned_list.append(
            serve_one(
                lax.all_to_all(
                    outgoing[step_index : step_index + 1],
                    "adapter",
                    split_axis=1,
                    concat_axis=1,
                    tiled=True,
                ),
                stack_down=stack_down[step_index : step_index + 1],
                stack_up=stack_up[step_index : step_index + 1],
            )
        )
    returned_rows = jnp.concatenate(returned_list, axis=0)
    delta_list = []
    for step_index in range(step_count):
        flat_rows = returned_rows[step_index].reshape(slot_count, model_width)
        delta_list.append(
            jnp.dot(placements[step_index], flat_rows, preferred_element_type=jnp.float32).astype(
                jnp.bfloat16
            )
        )
    return jnp.stack(delta_list)


def solution(mesh):
    return jax.shard_map(
        body,
        mesh=mesh,
        in_specs=(
            P(None, ("dp", "adapter"), None),
            P(None, ("dp", "adapter"), None),
            P(("dp", "adapter"), None, None),
            P(("dp", "adapter"), None, None),
            P(),
        ),
        out_specs=P(None, ("dp", "adapter"), None),
        check_vma=False,
    )
```

profile of v0, /device:TPU:0, one launch (start us, length us, event | category | flops | bytes accessed | tf_op | source)
XLA Modules:
  0.0 222.1 jit_solution(10519682711103507936)
XLA Ops:
  6.5 1.4 constant_dynamic-slice_fusion.1
  9.3 3.7 %select_bitcast_fusion.2 = (bf16[64,8192]{1,0:T(8,128)(2,1)}, bf16[64,8192]{1,0:T(8,128)(2,1)}, bf16[64,8192]{1,0:T(8,128)(2,1)}, bf16[64,8192]{1,0:T(8,128)(2,1)}) fusion(bf16[1,64,8192]{2,1,0:T(8,128)(2,1)} %param.8, pred[]{:T(512)S(6)} %eq.66, pred[]{:T(512)S(6)} %eq.73, bf16[1,64,8192]{2,1,0:T(8,128)(2,1)} %param.7), kind=kLoop, calls=%fused_computation.25 | loop fusion | flops 2097152 | bytes 6291458 | tf_op jit(solution)/shard_map/jit(_where)/select_n | solution.py:9
  13.0 0.7 copy-done.2
  13.6 0.1 fusion.23
  13.7 0.1 reduce_window_sum.17
  13.8 0.1 fusion.22
  13.8 0.1 reduce_window_sum.18
  13.9 0.2 select_reduce_fusion
  14.1 0.1 copy-done
  14.2 1.6 fusion
  15.8 5.2 %all-to-all-start = ((bf16[1,8,8,8192]{3,2,0,1:T(8,128)(2,1)}), bf16[1,8,8,8192]{3,2,0,1:T(8,128)(2,1)S(1)}, u32[]{:S(2)}, u32[]{:S(2)}) async-start(bf16[1,8,8,8192]{3,2,0,1:T(8,128)(2,1)} %fusion), calls=%async_computation | async-start | bytes 2097152 | tf_op jit(solution)/shard_map/all_to_all | solution.py:72
  21.0 1.6 fusion.2
  22.5 13.8 %all-to-all-done = bf16[1,8,8,8192]{3,2,0,1:T(8,128)(2,1)S(1)} async-done(((bf16[1,8,8,8192]{3,2,0,1:T(8,128)(2,1)}), bf16[1,8,8,8192]{3,2,0,1:T(8,128)(2,1)S(1)}, u32[]{:S(2)}, u32[]{:S(2)}) %all-to-all-start) | async-done | bytes 1048608 | tf_op jit(solution)/shard_map/all_to_all | solution.py:72
  36.4 3.6 %all-to-all-start.2 = ((bf16[1,8,8,8192]{3,2,0,1:T(8,128)(2,1)}), bf16[1,8,8,8192]{3,2,0,1:T(8,128)(2,1)S(1)}, u32[]{:S(2)}, u32[]{:S(2)}) async-start(bf16[1,8,8,8192]{3,2,0,1:T(8,128)(2,1)} %fusion.2), calls=%async_computation.2 | async-start | bytes 2097152 | tf_op jit(solution)/shard_map/all_to_all | solution.py:72
  39.9 131.9 %all-reduce.3.cloned.1.call-done = (bf16[64,8192]{1,0:T(8,128)(2,1)}, bf16[64,8192]{1,0:T(8,128)(2,1)}, bf16[64,8192]{1,0:T(8,128)(2,1)}, bf16[64,8192]{1,0:T(8,128)(2,1)}) async-done(((bf16[64,8192]{1,0:T(8,128)(2,1)}, bf16[64,8192]{1,0:T(8,128)(2,1)}, bf16[64,8192]{1,0:T(8,128)(2,1)}, bf16[64,8192]{1,0:T(8,128)(2,1)}), (bf16[64,8192]{1,0:T(8,128)(2,1)}, bf16[64,8192]{1,0:T(8,128)(2,1)}, ...) | async-done | bytes 4194320 | tf_op jit(solution)/shard_map/psum | solution.py:9
  171.9 3.8 %fusion.1 = bf16[1,8,8,8192]{3,2,0,1:T(8,128)(2,1)} fusion(bf16[64,8192]{1,0:T(8,128)(2,1)} %get-tuple-element.7, bf16[64,8192]{1,0:T(8,128)(2,1)} %get-tuple-element.8, bf16[1,8,8,8192]{3,2,0,1:T(8,128)(2,1)S(1)} %all-to-all-done), kind=kOutput, calls=%fused_computation.5 | convolution fusion | flops 134746112 | bytes 4194304 | tf_op jit(solution)/shard_map/scnr,srd->scnd/dot_general | solution.py:25
  175.7 3.8 %all-to-all-start.1 = ((bf16[1,8,8,8192]{3,2,0,1:T(8,128)(2,1)}), bf16[1,8,8,8192]{3,2,0,1:T(8,128)(2,1)S(1)}, u32[]{:S(2)}, u32[]{:S(2)}) async-start(bf16[1,8,8,8192]{3,2,0,1:T(8,128)(2,1)} %fusion.1), calls=%async_computation.1 | async-start | bytes 2097152 | tf_op jit(solution)/shard_map/all_to_all | solution.py:32
  179.5 3.5 %fusion.3 = bf16[1,8,8,8192]{3,2,0,1:T(8,128)(2,1)} fusion(bf16[64,8192]{1,0:T(8,128)(2,1)S(1)} %copy-done.1, bf16[64,8192]{1,0:T(8,128)(2,1)} %get-tuple-element.6, bf16[1,8,8,8192]{3,2,0,1:T(8,128)(2,1)S(1)} %all-to-all-done.2), kind=kOutput, calls=%fused_computation.7 | convolution fusion | flops 134746112 | bytes 4194304 | tf_op jit(solution)/shard_map/scnr,srd->scnd/dot_general | solution.py:25
  183.0 11.9 %all-to-all-done.1 = bf16[1,8,8,8192]{3,2,0,1:T(8,128)(2,1)S(1)} async-done(((bf16[1,8,8,8192]{3,2,0,1:T(8,128)(2,1)}), bf16[1,8,8,8192]{3,2,0,1:T(8,128)(2,1)S(1)}, u32[]{:S(2)}, u32[]{:S(2)}) %all-to-all-start.1) | async-done | bytes 1048608 | tf_op jit(solution)/shard_map/all_to_all | solution.py:32
  194.9 3.6 %all-to-all-start.3 = ((bf16[1,8,8,8192]{3,2,0,1:T(8,128)(2,1)}), bf16[1,8,8,8192]{3,2,0,1:T(8,128)(2,1)S(1)}, u32[]{:S(2)}, u32[]{:S(2)}) async-start(bf16[1,8,8,8192]{3,2,0,1:T(8,128)(2,1)} %fusion.3), calls=%async_computation.3 | async-start | bytes 2097152 | tf_op jit(solution)/shard_map/all_to_all | solution.py:32
  198.5 0.4 fusion.4
  198.9 15.0 %all-to-all-done.3 = bf16[1,8,8,8192]{3,2,0,1:T(8,128)(2,1)S(1)} async-done(((bf16[1,8,8,8192]{3,2,0,1:T(8,128)(2,1)}), bf16[1,8,8,8192]{3,2,0,1:T(8,128)(2,1)S(1)}, u32[]{:S(2)}, u32[]{:S(2)}) %all-to-all-start.3) | async-done | bytes 1048608 | tf_op jit(solution)/shard_map/all_to_all | solution.py:32
  213.8 0.3 fusion.5
  214.2 1.1 pad_maximum_fusion
  (9 shorter events, 0.0 us)
Async XLA Ops:
  6.5 165.3 %all-reduce.3.cloned.1.call-start = ((), (), s32[]{:S(2)}) async-start(), calls=%async_computation.4 | async-start | bytes 8388608 | tf_op jit(solution)/shard_map/psum | solution.py:9
  13.0 0.7 copy-start.2
  13.0 1.2 copy-start
  15.8 20.6 %all-to-all-start = ((bf16[1,8,8,8192]{3,2,0,1:T(8,128)(2,1)}), bf16[1,8,8,8192]{3,2,0,1:T(8,128)(2,1)S(1)}, u32[]{:S(2)}, u32[]{:S(2)}) async-start(bf16[1,8,8,8192]{3,2,0,1:T(8,128)(2,1)} %fusion), calls=%async_computation | async-start | bytes 2097152 | tf_op jit(solution)/shard_map/all_to_all | solution.py:72
  36.4 139.3 %all-to-all-start.2 = ((bf16[1,8,8,8192]{3,2,0,1:T(8,128)(2,1)}), bf16[1,8,8,8192]{3,2,0,1:T(8,128)(2,1)S(1)}, u32[]{:S(2)}, u32[]{:S(2)}) async-start(bf16[1,8,8,8192]{3,2,0,1:T(8,128)(2,1)} %fusion.2), calls=%async_computation.2 | async-start | bytes 2097152 | tf_op jit(solution)/shard_map/all_to_all | solution.py:72
  175.7 3.8 %copy-start.1 = (bf16[64,8192]{1,0:T(8,128)(2,1)S(1)}, bf16[64,8192]{1,0:T(8,128)(2,1)}, u32[]{:S(2)}) copy-start(bf16[64,8192]{1,0:T(8,128)(2,1)} %get-tuple-element.5) | copy-start | bytes 3145732
  175.7 19.2 %all-to-all-start.1 = ((bf16[1,8,8,8192]{3,2,0,1:T(8,128)(2,1)}), bf16[1,8,8,8192]{3,2,0,1:T(8,128)(2,1)S(1)}, u32[]{:S(2)}, u32[]{:S(2)}) async-start(bf16[1,8,8,8192]{3,2,0,1:T(8,128)(2,1)} %fusion.1), calls=%async_computation.1 | async-start | bytes 2097152 | tf_op jit(solution)/shard_map/all_to_all | solution.py:32
  194.9 18.9 %all-to-all-start.3 = ((bf16[1,8,8,8192]{3,2,0,1:T(8,128)(2,1)}), bf16[1,8,8,8192]{3,2,0,1:T(8,128)(2,1)S(1)}, u32[]{:S(2)}, u32[]{:S(2)}) async-start(bf16[1,8,8,8192]{3,2,0,1:T(8,128)(2,1)} %fusion.3), calls=%async_computation.3 | async-start | bytes 2097152 | tf_op jit(solution)/shard_map/all_to_all | solution.py:32
Sparse Core Ops, SparseCore 0:
  13.1 158.7 all-reduce.2
where the time goes:
time: 223 us; the launch traced here: 222 us
  waiting for transfers between devices  173 us (78%)
  starting transfers between devices  16.1 us (7%)
  between operations  14.8 us (7%)
  matrix products  11.2 us (5%)
  other arithmetic  5.16 us (2%)
    psum x1, waiting for transfers between devices, from_root(): return lax.psum(jnp.where(mine, array, jnp.zeros_like(array)), axis)  132 us
    all_to_all x2, waiting for transfers between devices, serve_one(): lax.all_to_all(result, 'adapter', split_axis=1, concat_axis=1, tiled=True)  26.9 us
    all_to_all x2, waiting for transfers between devices, body(): lax.all_to_all(outgoing[step_index:step_index + 1], 'adapter', split_axis...  13.9 us
    all_to_all x2, starting transfers between devices, body(): lax.all_to_all(outgoing[step_index:step_index + 1], 'adapter', split_axis...  8.73 us
    all_to_all x2, starting transfers between devices, serve_one(): lax.all_to_all(result, 'adapter', split_axis=1, concat_axis=1, tiled=True)  7.39 us
    dot_general x2, matrix products, project(): jnp.einsum('scnr,srd->scnd', low_rank, stack_up, preferred_element_type=j...  7.33 us
  transfers between devices with their start and end apart: 5, of which 4 were waited for; matrix products, arithmetic and copies ran while one was open for 5% of the time, Pallas kernels for 0%

commit v1 on v0

v1 whole, which is shorter than its diff:
```python
import functools

import jax
import jax.numpy as jnp
from jax import lax
from jax.experimental import pallas as pl
from jax.experimental.pallas import tpu as pltpu
from jax.sharding import PartitionSpec as P

MESH = pl.DeviceIdType.MESH
F32 = jnp.float32
BF16 = jnp.bfloat16
WIDTH = 512
SKEW = 2
LAG = 2


def kernel(
    n, cols, steps, cap, block, wc,
    owner_ref, slot_ref, states_ref, down_ref, up_ref, out_ref,
    below, above, xout, arrived, dout, returned, low_acc, low, pack, unpack,
    up_send, dn_send, x_send, d_send, below_sem, above_sem, x_sem, d_sem,
):
    z = lax.axis_index("dp")
    me = lax.axis_index("adapter")
    rows = states_ref.shape[1]
    rank = down_ref.shape[1]
    nw = states_ref.shape[2] // wc
    nch = 2 * nw
    slots = cols * block
    not_first = z > 0
    not_last = z < n - 1

    def lanes(w):
        return pl.ds(pl.multiple_of(w * wc, wc), wc)

    def block_rows(j):
        return pl.ds(pl.multiple_of(j * block, block), block)

    barrier = pltpu.get_barrier_semaphore()
    for o in range(1, cols):
        pl.semaphore_signal(
            barrier, inc=1, device_id={"adapter": lax.rem(me + o, cols)}, device_id_type=MESH
        )

    @pl.when(not_first)
    def _():
        pl.semaphore_signal(barrier, inc=1, device_id={"dp": z - 1}, device_id_type=MESH)

    @pl.when(not_last)
    def _():
        pl.semaphore_signal(barrier, inc=1, device_id={"dp": z + 1}, device_id_type=MESH)

    r_sub = lax.broadcasted_iota(jnp.int32, (rows, rows), 0)
    r_lane = lax.broadcasted_iota(jnp.int32, (rows, rows), 1)
    for s in range(steps):
        crow = slot_ref[s : s + 1, :]
        crow_b = jnp.broadcast_to(crow, (rows, rows))
        ccol = jnp.sum(jnp.where(r_sub == r_lane, crow_b, 0), axis=1, keepdims=True)
        same = jnp.broadcast_to(ccol, (rows, rows)) == crow_b
        rank_row = jnp.sum(jnp.where(same & (r_sub < r_lane), 1, 0), axis=0, keepdims=True)
        rank_col = jnp.sum(jnp.where(same & (r_lane < r_sub), 1, 0), axis=1, keepdims=True)
        trow = crow * block + s * cap + rank_row
        tcol = ccol * block + s * cap + rank_col
        pack[s] = jnp.where(
            lax.broadcasted_iota(jnp.int32, (slots, rows), 0) == trow, 1.0, 0.0
        ).astype(BF16)
        unpack[s] = jnp.where(
            lax.broadcasted_iota(jnp.int32, (rows, slots), 1) == tcol, 1.0, 0.0
        ).astype(BF16)
    low_acc[...] = jnp.zeros_like(low_acc)

    owners = [owner_ref[s, me] for s in range(steps)]
    pl.semaphore_wait(
        barrier, cols - 1 + not_first.astype(jnp.int32) + not_last.astype(jnp.int32)
    )

    def put_own(buf, k, merge):
        def go(src, w):
            mine = src[0, :, lanes(w)]
            for s in range(steps):
                part = pl.ds(s * rank, rank)
                if merge:
                    buf[k, part, :] = lax.select_n(owners[s] == z, buf[k, part, :], mine)
                else:
                    buf[k, part, :] = mine

        @pl.when(k < nw)
        def _():
            go(down_ref, k)

        @pl.when(k >= nw)
        def _():
            go(up_ref, k - nw)

    def hop(buf, k, has_in, has_out, target, recv_sem, send_sem):
        copy = pltpu.make_async_remote_copy(
            src_ref=buf.at[k],
            dst_ref=buf.at[k],
            send_sem=send_sem,
            recv_sem=recv_sem.at[k],
            device_id={"dp": target},
            device_id_type=MESH,
        )

        @pl.when(has_in)
        def _():
            copy.wait_recv()
            put_own(buf, k, True)

        @pl.when(jnp.logical_not(has_in))
        def _():
            put_own(buf, k, False)

        @pl.when(has_out)
        def _():
            copy.start()

    def exchange(src, dst, w, send_sem, recv_sem):
        dst[w, block_rows(me), :] = src[w, block_rows(me), :]
        for o in range(1, cols):
            peer = lax.rem(me + o, cols)
            pltpu.make_async_remote_copy(
                src_ref=src.at[w, block_rows(peer)],
                dst_ref=dst.at[w, block_rows(me)],
                send_sem=send_sem,
                recv_sem=recv_sem.at[w],
                device_id={"adapter": peer},
                device_id_type=MESH,
            ).start()

    def wait_exchange(dst, w, recv_sem):
        part = dst.at[w, pl.ds(0, slots - block)]
        pltpu.make_async_copy(part, part, recv_sem.at[w]).wait()

    def chosen(k):
        parts = []
        for s in range(steps):
            part = pl.ds(s * rank, rank)
            parts.append(lax.select_n(owners[s] <= z, above[k, part, :], below[k, part, :]))
        return jnp.concatenate(parts, axis=0)

    def iteration(i, carry):
        k_up = i - SKEW * z
        k_dn = i - SKEW * (n - 1 - z)

        @pl.when((k_up >= 0) & (k_up < nch))
        def _():
            hop(below, k_up, not_first, not_last, lax.rem(z + 1, n), below_sem, up_send)

        @pl.when((k_dn >= 0) & (k_dn < nch))
        def _():
            hop(above, k_dn, not_last, not_first, lax.rem(z + n - 1, n), above_sem, dn_send)

        @pl.when(i < nw)
        def _():
            total = jnp.zeros((slots, wc), F32)
            for s in range(steps):
                total = total + jnp.dot(
                    pack[s], states_ref[s, :, lanes(i)], preferred_element_type=F32
                )
            xout[i] = total.astype(BF16)
            exchange(xout, arrived, i, x_send, x_sem)

        k = i - SKEW * (n - 1)

        @pl.when((k >= 0) & (k < nw))
        def _():
            wait_exchange(arrived, k, x_sem)
            low_acc[...] += lax.dot_general(
                arrived[k], chosen(k), (((1,), (1,)), ((), ())), preferred_element_type=F32
            )

        @pl.when(k == nw - 1)
        def _():
            of_row = lax.rem(lax.broadcasted_iota(jnp.int32, low.shape, 0), block) // cap
            of_col = lax.broadcasted_iota(jnp.int32, low.shape, 1) // rank
            low[...] = jnp.where(of_row == of_col, low_acc[...], 0.0).astype(BF16)

        @pl.when((k >= nw) & (k < nch))
        def _():
            w = k - nw
            dout[w] = jnp.dot(low[...], chosen(k), preferred_element_type=F32).astype(BF16)
            exchange(dout, returned, w, d_send, d_sem)

        w_out = k - nw - LAG

        @pl.when((w_out >= 0) & (w_out < nw))
        def _():
            wait_exchange(returned, w_out, d_sem)
            for s in range(steps):
                out_ref[s, :, lanes(w_out)] = jnp.dot(
                    unpack[s], returned[w_out], preferred_element_type=F32
                ).astype(BF16)

        return carry

    lax.fori_loop(0, nch + SKEW * (n - 1) + LAG, iteration, 0)

    @pl.when(not_last)
    def _():
        pltpu.make_async_copy(below, below, up_send).wait()

    @pl.when(not_first)
    def _():
        pltpu.make_async_copy(above, above, dn_send).wait()

    for buf, sem in ((xout, x_send), (dout, d_send)):
        part = buf.at[:, pl.ds(0, slots - block)]
        pltpu.make_async_copy(part, part, sem).wait()


def body(n, cols, states, request_slot_index, down_weights, up_weights, active_adapter_owner):
    steps, rows, width = states.shape
    rank = down_weights.shape[1]
    cap = max(2, 2 * rows // cols)
    block = -(-steps * cap // 16) * 16
    slots = cols * block
    wc = min(WIDTH, width)
    nw = width // wc
    vmem = pl.BlockSpec(memory_space=pltpu.VMEM)
    dma = pltpu.SemaphoreType.DMA
    return pl.pallas_call(
        functools.partial(kernel, n, cols, steps, cap, block, wc),
        out_shape=jax.ShapeDtypeStruct(states.shape, states.dtype),
        in_specs=[pl.BlockSpec(memory_space=pltpu.SMEM)] + [vmem] * 4,
        out_specs=vmem,
        scratch_shapes=[
            pltpu.VMEM((2 * nw, steps * rank, wc), BF16),
            pltpu.VMEM((2 * nw, steps * rank, wc), BF16),
            pltpu.VMEM((nw, slots, wc), BF16),
            pltpu.VMEM((nw, slots, wc), BF16),
            pltpu.VMEM((nw, slots, wc), BF16),
            pltpu.VMEM((nw, slots, wc), BF16),
            pltpu.VMEM((slots, steps * rank), F32),
            pltpu.VMEM((slots, steps * rank), BF16),
            pltpu.VMEM((steps, slots, rows), BF16),
            pltpu.VMEM((steps, rows, slots), BF16),
            dma, dma, dma, dma,
            dma((2 * nw,)), dma((2 * nw,)), dma((nw,)), dma((nw,)),
        ],
        compiler_params=pltpu.CompilerParams(
            collective_id=0, has_side_effects=True, vmem_limit_bytes=56 * 1024 * 1024
        ),
    )(active_adapter_owner, request_slot_index[:, :, 0], states, down_weights, up_weights)


def solution(mesh):
    return jax.shard_map(
        functools.partial(body, mesh.shape["dp"], mesh.shape["adapter"]),
        mesh=mesh,
        in_specs=(
            P(None, ("dp", "adapter"), None),
            P(None, ("dp", "adapter"), None),
            P(("dp", "adapter"), None, None),
            P(("dp", "adapter"), None, None),
            P(),
        ),
        out_specs=P(None, ("dp", "adapter"), None),
        check_vma=False,
    )
```

time: 223 us -> 116 us (0.52)
  waiting for transfers between devices: 173 us -> 0 us
  Pallas kernels: 0 us -> 113 us
  starting transfers between devices: 16.1 us -> 0 us
  between operations: 14.8 us -> 0.01 us
  matrix products: 11.2 us -> 0 us
  other arithmetic: 5.16 us -> 0 us
    psum x1 -> x0, waiting for transfers between devices: 132 us -> none  [from_root(): return lax.psum(jnp.where(mine, array, jnp.zeros_like(array)), axis)]
    pallas_call x0 -> x1, Pallas kernels: none -> 113 us  [body(): pl.pallas_call(functools.partial(kernel, n, cols, steps, cap, block, wc),...]
    all_to_all x4 -> x0, waiting for transfers between devices: 40.7 us -> none  [the longest x2 26.9 us: serve_one(): lax.all_to_all(result, 'adapter', split_axis=1, concat_axis=1, tiled=True)]
    all_to_all x4 -> x0, starting transfers between devices: 16.1 us -> none  [the longest x2 8.73 us: body(): lax.all_to_all(outgoing[step_index:step_index + 1], 'adapter', split_axis...]
    dot_general x6 -> x0, matrix products: 11.2 us -> none  [the longest x2 7.33 us: project(): jnp.einsum('scnr,srd->scnd', low_rank, stack_up, preferred_element_type=j...]
    select_n x1 -> x0, other arithmetic: 3.65 us -> none  [from_root(): return lax.psum(jnp.where(mine, array, jnp.zeros_like(array)), axis)]
  transfers between devices with their start and end apart: 5 -> 0, of which waited for: 4 -> 0; matrix products, arithmetic and copies ran while one was open for 5% -> 0% of each run, Pallas kernels for 0% -> 0%
where the time goes in v1:
time: 116 us
  Pallas kernels  113 us (97%)
  local copies, waits for them, and re-layouts  2.26 us (2%)
    pallas_call x1, Pallas kernels, body(): pl.pallas_call(functools.partial(kernel, n, cols, steps, cap, block, wc),...  113 us

profile of v1, /device:TPU:0, one launch (start us, length us, event | category | flops | bytes accessed | tf_op | source)
XLA Modules:
  0.0 115.7 jit_solution(2402096260434554224)
XLA Ops:
  0.0 113.4 %shard_map.55 = bf16[2,32,8192]{2,1,0:T(8,128)(2,1)} custom-call(s32[2,8]{1,0:T(2,128)} %owner_ref.1, s32[2,32]{1,0:T(2,128)} %bitcast.1, bf16[2,32,8192]{2,1,0:T(8,128)(2,1)} %states_ref.1, bf16[1,64,8192]{2,1,0:T(8,128)(2,1)} %down_ref.1, bf16[1,64,8192]{2,1,0:T(8,128)(2,1)} %up_ref.1), custom_call_target="tpu_custom_call" | custom-call | tf_op jit(solution)/shard_map/pallas_call | solution.py:223
  113.4 2.3 %copy.7 = bf16[2,32,8192]{2,1,0:T(8,128)(2,1)} copy(bf16[2,32,8192]{2,1,0:T(8,128)(2,1)} %shard_map.55) | data formatting | bytes 2097152

commit v2 on v1

v2 whole, which is shorter than its diff:
```python
import functools

import jax
import jax.numpy as jnp
from jax import lax
from jax.experimental import pallas as pl
from jax.experimental.pallas import tpu as pltpu
from jax.sharding import PartitionSpec as P

MESH = pl.DeviceIdType.MESH
F32 = jnp.float32
BF16 = jnp.bfloat16
WIDTH = 256
SKEW = 3
LAG = 2
GROUP = 2


def kernel(
    n, cols, steps, cap, block, wc, group,
    owner_ref, slot_ref, states_any, down_any, up_any, out_ref,
    states_ref, down_ref, up_ref, below, above, xout, arrived, dout, returned, low_acc, low, pack, unpack,
    in_sem, up_send, dn_send, x_send, d_send, below_sem, above_sem, x_sem, d_sem,
):
    z = lax.axis_index("dp")
    me = lax.axis_index("adapter")
    rows = states_any.shape[1]
    rank = down_any.shape[1]
    nw = states_any.shape[2] // wc
    nch = 2 * nw
    slots = cols * block
    not_first = z > 0
    not_last = z < n - 1

    pieces = nw // group
    pw = wc * group
    loads = [
        pltpu.make_async_copy(src, dst, in_sem.at[i])
        for i, (src, dst) in enumerate(
            ((down_any, down_ref), (up_any, up_ref), (states_any, states_ref))
        )
    ]
    for load in loads:
        load.start()

    def lanes(w):
        return pl.ds(pl.multiple_of(w * wc, wc), wc)

    def piece_lanes(p):
        return pl.ds(pl.multiple_of(p * pw, pw), pw)

    def block_rows(j):
        return pl.ds(pl.multiple_of(j * block, block), block)

    barrier = pltpu.get_barrier_semaphore()
    for o in range(1, cols):
        pl.semaphore_signal(
            barrier, inc=1, device_id={"adapter": lax.rem(me + o, cols)}, device_id_type=MESH
        )

    @pl.when(not_first)
    def _():
        pl.semaphore_signal(barrier, inc=1, device_id={"dp": z - 1}, device_id_type=MESH)

    @pl.when(not_last)
    def _():
        pl.semaphore_signal(barrier, inc=1, device_id={"dp": z + 1}, device_id_type=MESH)

    r_sub = lax.broadcasted_iota(jnp.int32, (rows, rows), 0)
    r_lane = lax.broadcasted_iota(jnp.int32, (rows, rows), 1)
    for s in range(steps):
        crow = slot_ref[s : s + 1, :]
        crow_b = jnp.broadcast_to(crow, (rows, rows))
        ccol = jnp.sum(jnp.where(r_sub == r_lane, crow_b, 0), axis=1, keepdims=True)
        same = jnp.broadcast_to(ccol, (rows, rows)) == crow_b
        rank_row = jnp.sum(jnp.where(same & (r_sub < r_lane), 1, 0), axis=0, keepdims=True)
        rank_col = jnp.sum(jnp.where(same & (r_lane < r_sub), 1, 0), axis=1, keepdims=True)
        trow = crow * block + s * cap + rank_row
        tcol = ccol * block + s * cap + rank_col
        pack[s] = jnp.where(
            lax.broadcasted_iota(jnp.int32, (slots, rows), 0) == trow, 1.0, 0.0
        ).astype(BF16)
        unpack[s] = jnp.where(
            lax.broadcasted_iota(jnp.int32, (rows, slots), 1) == tcol, 1.0, 0.0
        ).astype(BF16)
    low_acc[...] = jnp.zeros_like(low_acc)

    owners = [owner_ref[s, me] for s in range(steps)]
    for load in loads:
        load.wait()
    pl.semaphore_wait(
        barrier, cols - 1 + not_first.astype(jnp.int32) + not_last.astype(jnp.int32)
    )

    def own(k, use):
        @pl.when(k < nw)
        def _():
            use(down_ref[0, :, lanes(k)])

        @pl.when(k >= nw)
        def _():
            use(up_ref[0, :, lanes(k - nw)])

    def part(s):
        return pl.ds(s * rank, rank)

    def hop(buf, i, place, owner_places, target, recv_sem, send_sem):
        def copy(k, src, dst):
            return pltpu.make_async_remote_copy(
                src_ref=buf.at[k, src],
                dst_ref=buf.at[k, dst],
                send_sem=send_sem,
                recv_sem=recv_sem.at[k],
                device_id={"dp": target},
                device_id_type=MESH,
            )

        whole = pl.ds(0, steps * rank)
        second = i - SKEW
        later = i - SKEW * place

        @pl.when((place == 0) & (i < nch))
        def _():
            def use(mine):
                for s in range(steps):
                    buf[i, part(s), :] = mine

            own(i, use)
            copy(i, part(0), part(1)).start()

        @pl.when((place == 1) & (i < nch))
        def _():
            def use(mine):
                buf[i, part(0), :] = mine

            own(i, use)

            @pl.when(place < n - 1)
            def _():
                copy(i, part(0), part(0)).start()

        @pl.when((place == 1) & (second >= 0) & (second < nch))
        def _():
            copy(second, part(1), part(1)).wait_recv()

            @pl.when(place < n - 1)
            def _():
                copy(second, part(1), part(1)).start()

        @pl.when((place > 1) & (later >= 0) & (later < nch))
        def _():
            copy(later, whole, whole).wait_recv()

            def use(mine):
                theirs = [buf[later, part(s), :] for s in range(steps)]
                for s in range(steps):
                    value = theirs[s]
                    raw = place == 2
                    if s == 0:
                        value = lax.select_n(raw & (owner_places[s] == 0), value, theirs[1])
                    else:
                        value = lax.select_n(raw & (owner_places[s] == 0), value, theirs[1])
                        value = lax.select_n(raw & (owner_places[s] == 1), value, theirs[0])
                    buf[later, part(s), :] = lax.select_n(owner_places[s] == place, value, mine)

            own(later, use)

            @pl.when(place < n - 1)
            def _():
                copy(later, whole, whole).start()

    def wait_sent(buf, place, send_sem):
        @pl.when(place == 0)
        def _():
            sent = buf.at[:, part(0)]
            pltpu.make_async_copy(sent, sent, send_sem).wait()

        @pl.when((place > 0) & (place < n - 1))
        def _():
            pltpu.make_async_copy(buf, buf, send_sem).wait()

    def exchange(src, dst, w, send_sem, recv_sem):
        dst[w, block_rows(me), :] = src[w, block_rows(me), :]
        for o in range(1, cols):
            peer = lax.rem(me + o, cols)
            pltpu.make_async_remote_copy(
                src_ref=src.at[w, block_rows(peer)],
                dst_ref=dst.at[w, block_rows(me)],
                send_sem=send_sem,
                recv_sem=recv_sem.at[w],
                device_id={"adapter": peer},
                device_id_type=MESH,
            ).start()

    def wait_exchange(dst, w, recv_sem):
        remote = dst.at[w, pl.ds(0, slots - block)]
        pltpu.make_async_copy(remote, remote, recv_sem.at[w]).wait()

    ups = owners
    dns = [n - 1 - owner for owner in owners]

    def pick(buf, k, place, owner_places, s):
        other = (place == 1) & (owner_places[s] == (0 if s == 0 else 1))
        return lax.select_n(other, buf[k, part(s), :], buf[k, part(1 if s == 0 else 0), :])

    def chosen(k):
        parts = []
        for s in range(steps):
            parts.append(
                lax.select_n(
                    owners[s] <= z,
                    pick(above, k, n - 1 - z, dns, s),
                    pick(below, k, z, ups, s),
                )
            )
        return jnp.concatenate(parts, axis=0)

    def iteration(i, carry):
        hop(below, i, z, ups, lax.rem(z + 1, n), below_sem, up_send)
        hop(above, i, n - 1 - z, dns, lax.rem(z + n - 1, n), above_sem, dn_send)

        @pl.when((lax.rem(i, group) == 0) & (i < nw))
        def _():
            p = i // group
            total = jnp.zeros((slots, pw), F32)
            for s in range(steps):
                total = total + jnp.dot(
                    pack[s], states_ref[s, :, piece_lanes(p)], preferred_element_type=F32
                )
            xout[p] = total.astype(BF16)
            exchange(xout, arrived, p, x_send, x_sem)

        k = i - SKEW * (n - 1)

        @pl.when((k >= 0) & (k < nw) & (lax.rem(k, group) == 0))
        def _():
            wait_exchange(arrived, k // group, x_sem)

        @pl.when((k >= 0) & (k < nw))
        def _():
            low_acc[...] += lax.dot_general(
                arrived[k // group, :, lanes(lax.rem(k, group))],
                chosen(k),
                (((1,), (1,)), ((), ())),
                preferred_element_type=F32,
            )

        @pl.when(k == nw - 1)
        def _():
            of_row = lax.rem(lax.broadcasted_iota(jnp.int32, low.shape, 0), block) // cap
            of_col = lax.broadcasted_iota(jnp.int32, low.shape, 1) // rank
            low[...] = jnp.where(of_row == of_col, low_acc[...], 0.0).astype(BF16)

        @pl.when((k >= nw) & (k < nch))
        def _():
            w = k - nw
            dout[w // group, :, lanes(lax.rem(w, group))] = jnp.dot(
                low[...], chosen(k), preferred_element_type=F32
            ).astype(BF16)

        @pl.when((k >= nw) & (k < nch) & (lax.rem(k - nw, group) == group - 1))
        def _():
            exchange(dout, returned, (k - nw) // group, d_send, d_sem)

        w_out = k - nw - LAG

        @pl.when((w_out >= 0) & (w_out < nw) & (lax.rem(w_out, group) == group - 1))
        def _():
            p = w_out // group
            wait_exchange(returned, p, d_sem)
            for s in range(steps):
                out_ref[s, :, piece_lanes(p)] = jnp.dot(
                    unpack[s], returned[p], preferred_element_type=F32
                ).astype(BF16)

        return carry

    lax.fori_loop(0, nch + SKEW * (n - 1) + LAG, iteration, 0)

    wait_sent(below, z, up_send)
    wait_sent(above, n - 1 - z, dn_send)
    for buf, sem in ((xout, x_send), (dout, d_send)):
        sent = buf.at[:, pl.ds(0, slots - block)]
        pltpu.make_async_copy(sent, sent, sem).wait()


def body(n, cols, states, request_slot_index, down_weights, up_weights, active_adapter_owner):
    steps, rows, width = states.shape
    rank = down_weights.shape[1]
    cap = max(2, 2 * rows // cols)
    block = -(-steps * cap // 16) * 16
    slots = cols * block
    wc = min(WIDTH, width)
    nw = width // wc
    group = GROUP if nw % GROUP == 0 else 1
    vmem = pl.BlockSpec(memory_space=pltpu.VMEM)
    hbm = pl.BlockSpec(memory_space=pl.ANY)
    dma = pltpu.SemaphoreType.DMA
    stream = pltpu.VMEM((2 * nw, steps * rank, wc), BF16)
    piece = pltpu.VMEM((nw // group, slots, wc * group), BF16)
    return pl.pallas_call(
        functools.partial(kernel, n, cols, steps, cap, block, wc, group),
        out_shape=pltpu.VMEM(states.shape, states.dtype),
        in_specs=[pl.BlockSpec(memory_space=pltpu.SMEM), vmem, hbm, hbm, hbm],
        out_specs=vmem,
        scratch_shapes=[
            pltpu.VMEM(states.shape, BF16),
            pltpu.VMEM(down_weights.shape, BF16),
            pltpu.VMEM(up_weights.shape, BF16),
            stream, stream, piece, piece, piece, piece,
            pltpu.VMEM((slots, steps * rank), F32),
            pltpu.VMEM((slots, steps * rank), BF16),
            pltpu.VMEM((steps, slots, rows), BF16),
            pltpu.VMEM((steps, rows, slots), BF16),
            dma((3,)), dma, dma, dma, dma,
            dma((2 * nw,)), dma((2 * nw,)), dma((nw // group,)), dma((nw // group,)),
        ],
        compiler_params=pltpu.CompilerParams(
            collective_id=0, has_side_effects=True, vmem_limit_bytes=56 * 1024 * 1024
        ),
    )(active_adapter_owner, request_slot_index[:, :, 0], states, down_weights, up_weights)


def solution(mesh):
    return jax.shard_map(
        functools.partial(body, mesh.shape["dp"], mesh.shape["adapter"]),
        mesh=mesh,
        in_specs=(
            P(None, ("dp", "adapter"), None),
            P(None, ("dp", "adapter"), None),
            P(("dp", "adapter"), None, None),
            P(("dp", "adapter"), None, None),
            P(),
        ),
        out_specs=P(None, ("dp", "adapter"), None),
        check_vma=False,
    )
```

time: 116 us -> 111 us (0.957)
  Pallas kernels: 113 us -> 110 us
  local copies, waits for them, and re-layouts: 2.26 us -> 0.97 us
    pallas_call x1, Pallas kernels: 113 us -> 110 us  [body(): pl.pallas_call(functools.partial(kernel, n, cols, steps, cap, block, wc,...]
    unnamed x1, local copies, waits for them, and re-layouts: 2.26 us -> 0.97 us
where the time goes in v2:
time: 111 us
  Pallas kernels  110 us (99%)
    pallas_call x1, Pallas kernels, body(): pl.pallas_call(functools.partial(kernel, n, cols, steps, cap, block, wc,...  110 us

profile of v2, /device:TPU:0, one launch (start us, length us, event | category | flops | bytes accessed | tf_op | source)
XLA Modules:
  0.0 111.0 jit_solution(8772925264493148426)
XLA Ops:
  0.0 110.0 %shard_map.55 = bf16[2,32,8192]{2,1,0:T(8,128)(2,1)S(1)} custom-call(s32[2,8]{1,0:T(2,128)} %owner_ref.1, s32[2,32]{1,0:T(2,128)} %bitcast.1, bf16[2,32,8192]{2,1,0:T(8,128)(2,1)} %states_any.1, bf16[1,64,8192]{2,1,0:T(8,128)(2,1)} %down_any.1, bf16[1,64,8192]{2,1,0:T(8,128)(2,1)} %up_any.1), custom_call_target="tpu_custom_call" | custom-call | tf_op jit(solution)/shard_map/pallas_call | solution.py:301
  110.0 1.0 copy.7

commit v3 on v2

--- a/solution.py
+++ b/solution.py
@@ -12,7 +12,7 @@
 BF16 = jnp.bfloat16
 WIDTH = 256
 SKEW = 3
-LAG = 2
+LAG = 3
 GROUP = 2
 
 
@@ -179,10 +179,16 @@
         def _():
             pltpu.make_async_copy(buf, buf, send_sem).wait()
 
+    partners = []
+    for o in range(cols - 1, 0, -1):
+        peer, bit = 0, 1
+        while bit < cols:
+            peer = peer + bit * lax.rem(lax.rem(me // bit, 2) + o // bit % 2, 2)
+            bit = 2 * bit
+        partners.append(peer if bit == cols else lax.rem(me + o, cols))
+
     def exchange(src, dst, w, send_sem, recv_sem):
-        dst[w, block_rows(me), :] = src[w, block_rows(me), :]
-        for o in range(1, cols):
-            peer = lax.rem(me + o, cols)
+        for peer in partners:
             pltpu.make_async_remote_copy(
                 src_ref=src.at[w, block_rows(peer)],
                 dst_ref=dst.at[w, block_rows(me)],
@@ -191,6 +197,7 @@
                 device_id={"adapter": peer},
                 device_id_type=MESH,
             ).start()
+        dst[w, block_rows(me), :] = src[w, block_rows(me), :]
 
     def wait_exchange(dst, w, recv_sem):
         remote = dst.at[w, pl.ds(0, slots - block)]

time: 111 us -> 110 us (level)
  no operation moved by 1% of the time
where the time goes in v3:
time: 110 us
  Pallas kernels  109 us (99%)
    pallas_call x1, Pallas kernels, body(): pl.pallas_call(functools.partial(kernel, n, cols, steps, cap, block, wc,...  109 us

profile of v3, /device:TPU:0, one launch (start us, length us, event | category | flops | bytes accessed | tf_op | source)
XLA Modules:
  0.0 110.2 jit_solution(13982114571289070070)
XLA Ops:
  0.0 109.2 %shard_map.55 = bf16[2,32,8192]{2,1,0:T(8,128)(2,1)S(1)} custom-call(s32[2,8]{1,0:T(2,128)} %owner_ref.1, s32[2,32]{1,0:T(2,128)} %bitcast.1, bf16[2,32,8192]{2,1,0:T(8,128)(2,1)} %states_any.1, bf16[1,64,8192]{2,1,0:T(8,128)(2,1)} %down_any.1, bf16[1,64,8192]{2,1,0:T(8,128)(2,1)} %up_any.1), custom_call_target="tpu_custom_call" | custom-call | tf_op jit(solution)/shard_map/pallas_call | solution.py:308
  109.2 1.0 copy.7

commit v4 on v3

--- a/solution.py
+++ b/solution.py
@@ -187,17 +187,17 @@
             bit = 2 * bit
         partners.append(peer if bit == cols else lax.rem(me + o, cols))
 
-    def exchange(src, dst, w, send_sem, recv_sem):
+    def exchange(src, dst, w, span, send_sem, recv_sem):
         for peer in partners:
             pltpu.make_async_remote_copy(
-                src_ref=src.at[w, block_rows(peer)],
-                dst_ref=dst.at[w, block_rows(me)],
+                src_ref=src.at[w, block_rows(peer), span],
+                dst_ref=dst.at[w, block_rows(me), span],
                 send_sem=send_sem,
                 recv_sem=recv_sem.at[w],
                 device_id={"adapter": peer},
                 device_id_type=MESH,
             ).start()
-        dst[w, block_rows(me), :] = src[w, block_rows(me), :]
+        dst[w, block_rows(me), span] = src[w, block_rows(me), span]
 
     def wait_exchange(dst, w, recv_sem):
         remote = dst.at[w, pl.ds(0, slots - block)]
@@ -235,7 +235,7 @@
                     pack[s], states_ref[s, :, piece_lanes(p)], preferred_element_type=F32
                 )
             xout[p] = total.astype(BF16)
-            exchange(xout, arrived, p, x_send, x_sem)
+            exchange(xout, arrived, p, pl.ds(0, pw), x_send, x_sem)
 
         k = i - SKEW * (n - 1)
 
@@ -265,9 +265,14 @@
                 low[...], chosen(k), preferred_element_type=F32
             ).astype(BF16)
 
-        @pl.when((k >= nw) & (k < nch) & (lax.rem(k - nw, group) == group - 1))
-        def _():
-            exchange(dout, returned, (k - nw) // group, d_send, d_sem)
+        @pl.when((k >= nw) & (k < nch - group) & (lax.rem(k - nw, group) == group - 1))
+        def _():
+            exchange(dout, returned, (k - nw) // group, pl.ds(0, pw), d_send, d_sem)
+
+        @pl.when((k >= nch - group) & (k < nch))
+        def _():
+            span = lanes(lax.rem(k - nw, group))
+            exchange(dout, returned, pieces - 1, span, d_send, d_sem)
 
         w_out = k - nw - LAG
 

time: 110 us -> 110 us (level)
  no operation moved by 1% of the time
where the time goes in v4:
time: 110 us
  Pallas kernels  109 us (99%)
    pallas_call x1, Pallas kernels, body(): pl.pallas_call(functools.partial(kernel, n, cols, steps, cap, block, wc,...  109 us

profile of v4, /device:TPU:0, one launch (start us, length us, event | category | flops | bytes accessed | tf_op | source)
XLA Modules:
  0.0 109.9 jit_solution(3581102268421506743)
XLA Ops:
  0.0 109.0 %shard_map.55 = bf16[2,32,8192]{2,1,0:T(8,128)(2,1)S(1)} custom-call(s32[2,8]{1,0:T(2,128)} %owner_ref.1, s32[2,32]{1,0:T(2,128)} %bitcast.1, bf16[2,32,8192]{2,1,0:T(8,128)(2,1)} %states_any.1, bf16[1,64,8192]{2,1,0:T(8,128)(2,1)} %down_any.1, bf16[1,64,8192]{2,1,0:T(8,128)(2,1)} %up_any.1), custom_call_target="tpu_custom_call" | custom-call | tf_op jit(solution)/shard_map/pallas_call | solution.py:313
  109.0 1.0 copy.7
